TPU v7x, 32 devices: a whole 2x2x4 slice. The times are simulated.
32 devices in a mesh: owner: 32 (over z, y, x, core).
Axes of the slice: x: 2, y: 2, z: 4, core: 2. Of those that a mesh axis runs over, the one named last changes fastest.
Arguments:
- frontier: bfloat16 [512, 1326], P('owner'), may hold values from 0.019897461 to 1
- policy_table: bfloat16 [2048, 1326], replicated, may hold values from 0.019897461 to 1
- first_counts: int32 [512], P('owner'), may hold values from 1 to 64
- policy_index: int32 [3, 16384], P(None, 'owner'), may hold values from 0 to 2047
- owner_index: int32 [3, 16384], P(None, 'owner'), may hold values from 0 to 31
- next_counts: int32 [2, 16384], P(None, 'owner'), may hold values from 0 to 64, as said below
- value_in: bfloat16 [1326, 1536], replicated, may hold values from -0.15625 to 0.15625
- value_out: bfloat16 [1536, 1326], replicated, may hold values from -0.15625 to 0.15625
Outputs:
- leaf_values: bfloat16 [3, 16384, 1326], P(None, 'owner')
Inputs may be any that keep to these rules, and one draw needn't show every extreme that they name: `next_counts`: 0 marks a belief that is not expanded.
All inputs are finite; a program needn't handle non-finite values.
Results may differ from a plain program's by a relative error of at most 0.0067.
Values may be sent and summed in bfloat16 or wider, within the bound.
A program may use at most 128 MiB of HBM per device.

v0:
```python
import jax
import jax.numpy as jnp
from jax import lax
from jax.experimental import pallas as pl
from jax.experimental.pallas import tpu as pltpu
from jax.sharding import PartitionSpec as P

LEVELS = 3
SLOTS = 512
RECV_DEV = 512
NODE_DEV = 384


def own_slots(owners, mine, capacity):
    slots = owners.shape[1]
    hit = owners == mine
    upper = jnp.triu(jnp.ones((slots, slots), jnp.bfloat16))
    count = jnp.dot(hit.astype(jnp.bfloat16), upper, preferred_element_type=jnp.float32).astype(
        jnp.int32
    )
    rank = jnp.where(hit, count - 1, -1)
    return rank[:, None, :] == jnp.arange(capacity, dtype=jnp.int32)[None, :, None]


def pick(onehot, values):
    return jnp.sum(jnp.where(onehot, values[:, None, :], 0), axis=2)


def step_place(step):
    level, begin = jnp.int32(0), jnp.int32(0)
    for depth in range(1, LEVELS):
        start = depth * (depth + 1) // 2
        level = jnp.where(step >= start, depth, level)
        begin = jnp.where(step >= start, start, begin)
    return level, step == begin, step == begin + level


def rebuild_kernel(
    index_ref,
    roots_hbm,
    table_hbm,
    in_hbm,
    out_hbm,
    values_ref,
    roots_ref,
    table_ref,
    in_ref,
    out_ref,
    rows_ref,
    sems,
):
    step = pl.program_id(0)
    level, first, last = step_place(step)
    copies = [
        pltpu.make_async_copy(source, target, sems.at[k])
        for k, (source, target) in enumerate(
            (
                (roots_hbm, roots_ref),
                (table_hbm, table_ref),
                (in_hbm, in_ref),
                (out_hbm, out_ref),
            )
        )
    ]

    @pl.when(step == 0)
    def _():
        for copy in copies:
            copy.start()
        copies[0].wait()
        copies[1].wait()

    index = index_ref[...]
    lane = lax.broadcasted_iota(jnp.int32, index.shape, 1)

    def column(place):
        return jnp.sum(jnp.where(lane == place, index, 0.0), axis=1, keepdims=True)

    def gathered(place, table):
        entry = lax.broadcasted_iota(jnp.int32, (index.shape[0], table.shape[0]), 1)
        onehot = jnp.where(entry.astype(jnp.float32) == column(place), 1.0, 0.0)
        return jnp.dot(
            onehot.astype(jnp.bfloat16), table[...], preferred_element_type=jnp.float32
        )

    root_place = LEVELS * (LEVELS + 1) // 2 + level

    @pl.when(first)
    def _():
        rows_ref[...] = gathered(root_place, roots_ref).astype(jnp.bfloat16)

    rows = rows_ref[...].astype(jnp.float32) * gathered(step, table_ref)
    mass = jnp.sum(rows, axis=1, keepdims=True)
    mass = jnp.where(column(root_place) >= 0.0, mass, 1.0)
    rows_ref[...] = (rows * (rows.shape[1] / mass)).astype(jnp.bfloat16)

    @pl.when(step == 0)
    def _():
        copies[2].wait()
        copies[3].wait()

    @pl.when(last)
    def _():
        hidden = jnp.dot(rows_ref[...], in_ref[...], preferred_element_type=jnp.float32)
        hidden = jnp.maximum(hidden, 0.0).astype(jnp.bfloat16)
        values = jnp.dot(hidden, out_ref[...], preferred_element_type=jnp.float32)
        values_ref[0] = values.astype(jnp.bfloat16)


def rebuild(index, roots, table, value_in, value_out):
    rows, hands = index.shape[0], table.shape[1]
    steps = LEVELS * (LEVELS + 1) // 2
    return pl.pallas_call(
        rebuild_kernel,
        grid=(steps,),
        out_shape=jax.ShapeDtypeStruct((LEVELS, rows, hands), jnp.bfloat16),
        in_specs=[pl.BlockSpec(index.shape, lambda step: (0, 0))]
        + [pl.BlockSpec(memory_space=pl.ANY)] * 4,
        out_specs=pl.BlockSpec((1, rows, hands), lambda step: (step_place(step)[0], 0, 0)),
        scratch_shapes=[
            pltpu.VMEM(array.shape, array.dtype) for array in (roots, table, value_in, value_out)
        ]
        + [pltpu.VMEM((rows, hands), jnp.bfloat16), pltpu.SemaphoreType.DMA((4,))],
        compiler_params=pltpu.CompilerParams(vmem_limit_bytes=56 * 1024 * 1024),
    )(index, roots, table, value_in, value_out)


def share(block):
    devices = lax.axis_size("owner")
    copies = jnp.broadcast_to(block[None], (devices,) + block.shape)
    return lax.all_to_all(copies, "owner", split_axis=0, concat_axis=0, tiled=True)


def on_device(
    frontier,
    policy_table,
    first_counts,
    policy_index,
    owner_index,
    next_counts,
    value_in,
    value_out,
):
    devices = lax.axis_size("owner")
    mine = lax.axis_index("owner")
    capacity = RECV_DEV // devices
    kept_limit = NODE_DEV * devices
    hands = frontier.shape[1]
    roots = share(frontier).reshape(-1, hands)
    meta = jnp.concatenate([owner_index, policy_index, next_counts], axis=0)
    meta = share(meta)
    counts = share(first_counts)
    lineage = [jnp.arange(roots.shape[0], dtype=jnp.int32).reshape(devices, -1)]
    columns, root_columns = [], []
    for depth in range(LEVELS):
        onehot = own_slots(meta[:, depth], mine, capacity)
        slot_index = jnp.arange(SLOTS, dtype=jnp.int32)[None, :]
        slot = pick(onehot, slot_index + 1) - 1
        policy = pick(onehot, meta[:, LEVELS + depth])
        ends = jnp.cumsum(counts, axis=1)
        totals = jnp.minimum(ends[:, -1], SLOTS)
        offsets = jnp.cumsum(totals) - totals
        kept = (slot >= 0) & (slot < totals[:, None]) & (offsets[:, None] + slot < kept_limit)
        parent = ((ends - counts)[:, None, :] <= slot[:, :, None]) & (
            slot[:, :, None] < ends[:, None, :]
        )
        lineage = [pick(parent, part) for part in lineage] + [policy]
        root_columns.append(jnp.where(kept, lineage[0], -1))
        columns += lineage[1:]
        if depth < LEVELS - 1:
            following = jnp.where(kept, pick(onehot, meta[:, 2 * LEVELS + depth]), 0)
            packed = jnp.stack([part.reshape(-1) for part in lineage + [following]])
            packed = share(packed)
            lineage = [packed[:, k] for k in range(len(lineage))]
            counts = packed[:, -1]
    index = jnp.stack([part.reshape(-1) for part in columns + root_columns], axis=1)
    return rebuild(index.astype(jnp.float32), roots, policy_table, value_in, value_out)


def solution(mesh):
    placed = (
        P("owner", None),
        P(),
        P("owner"),
        P(None, "owner"),
        P(None, "owner"),
        P(None, "owner"),
        P(),
        P(),
    )
    return jax.shard_map(
        on_device, mesh=mesh, in_specs=placed, out_specs=P(None, "owner", None), check_vma=False
    )
```

profile of v0, /device:TPU:0, one launch (start us, length us, event | category | flops | bytes accessed | tf_op | source)
XLA Modules:
  0.0 163.9 jit_solution(16142747991353144196)
XLA Ops:
  0.0 1.3 broadcast_in_dim.201
  1.3 7.3 %all-to-all-start.1 = ((s32[32,1,16]{2,1,0:T(1,128)}), s32[32,1,16]{2,1,0:T(1,128)S(1)}, u32[]{:S(2)}, u32[]{:S(2)}) async-start(s32[32,1,16]{2,1,0:T(1,128)} %broadcast_in_dim.201), calls=%async_computation.1 | async-start | bytes 32768 | tf_op jit(solution)/shard_map/all_to_all | solution.py:131
  8.6 0.7 pad_add_fusion
  9.3 6.4 %all-to-all-done.1 = s32[32,1,16]{2,1,0:T(1,128)S(1)} async-done(((s32[32,1,16]{2,1,0:T(1,128)}), s32[32,1,16]{2,1,0:T(1,128)S(1)}, u32[]{:S(2)}, u32[]{:S(2)}) %all-to-all-start.1) | async-done | bytes 2080 | tf_op jit(solution)/shard_map/all_to_all | solution.py:131
  15.7 0.9 broadcast_in_dim.196
  16.6 2.6 %all-to-all-start = ((s32[32,8,512]{2,1,0:T(8,128)}), s32[32,8,512]{2,1,0:T(8,128)S(1)}, u32[]{:S(2)}, u32[]{:S(2)}) async-start(s32[32,8,512]{2,1,0:T(8,128)} %broadcast_in_dim.196), calls=%async_computation | async-start | bytes 1048576 | tf_op jit(solution)/shard_map/all_to_all | solution.py:131
  19.2 0.2 reduce_window_sum.73
  19.7 0.2 fusion.41
  19.9 14.9 %all-to-all-done = s32[32,8,512]{2,1,0:T(8,128)S(1)} async-done(((s32[32,8,512]{2,1,0:T(8,128)}), s32[32,8,512]{2,1,0:T(8,128)S(1)}, u32[]{:S(2)}, u32[]{:S(2)}) %all-to-all-start) | async-done | bytes 524320 | tf_op jit(solution)/shard_map/all_to_all | solution.py:131
  34.8 0.4 fusion.44
  35.2 0.3 fusion.1
  35.4 0.3 fusion.3
  35.7 0.3 fusion.5
  36.0 4.5 %select_reduce_fusion.1 = (s32[32,16]{1,0:T(8,128)S(1)}, s32[32,16]{1,0:T(8,128)S(1)}, s32[32,16]{1,0:T(8,128)S(1)}, s32[32,16]{1,0:T(8,128)S(1)}, s32[32,16]{1,...) fusion(s32[32,512]{1,0:T(8,128)S(1)} %get-tuple-element.52, ...), kind=kLoop, calls=%fused_computation.10 | loop fusion | flops 4976640 | bytes 542720 | tf_op jit(solution)/shard_map/reduce_sum | solution.py:26
  40.5 0.1 stack_reshape.40
  40.8 0.1 stack_reshape.39
  41.0 0.1 reshape.466
  41.1 0.7 broadcast_in_dim.207
  41.8 2.9 %all-to-all-start.2 = ((s32[32,3,512]{2,1,0:T(4,128)}), s32[32,3,512]{2,1,0:T(4,128)S(1)}, u32[]{:S(2)}, u32[]{:S(2)}) async-start(s32[32,3,512]{2,1,0:T(4,128)} %broadcast_in_dim.207), calls=%async_computation.2 | async-start | bytes 524288 | tf_op jit(solution)/shard_map/all_to_all | solution.py:131
  44.7 0.1 stack_reshape.45
  44.8 10.5 %all-to-all-done.2 = s32[32,3,512]{2,1,0:T(4,128)S(1)} async-done(((s32[32,3,512]{2,1,0:T(4,128)}), s32[32,3,512]{2,1,0:T(4,128)S(1)}, u32[]{:S(2)}, u32[]{:S(2)}) %all-to-all-start.2) | async-done | bytes 196640 | tf_op jit(solution)/shard_map/all_to_all | solution.py:131
  55.3 0.1 fusion.46
  55.5 1.2 reduce-window.25
  56.6 0.2 slice_reduce_fusion.1
  56.9 0.1 copy_bitcast_fusion.1
  57.3 1.4 select_reduce_fusion.6
  58.7 0.1 stack_reshape.43
  58.9 0.2 fusion.42
  59.2 0.1 reshape.468
  59.3 12.8 %all_to_all.29 = s32[32,4,512]{2,1,0:T(4,128)S(1)} all-to-all(s32[32,4,512]{2,1,0:T(4,128)S(1)} %broadcast_in_dim.216), channel_id=1, replica_groups=mesh['owner'=32] {'owner'}, dimensions={0} | all-to-all | bytes 524288 | tf_op jit(solution)/shard_map/all_to_all | solution.py:131
  72.1 1.2 broadcast_in_dim.225
  73.3 2.9 %all-to-all-start.4 = ((bf16[32,16,1326]{2,1,0:T(8,128)(2,1)}), bf16[32,16,1326]{2,1,0:T(8,128)(2,1)S(1)}, u32[]{:S(2)}, u32[]{:S(2)}) async-start(bf16[32,16,1326]{2,1,0:T(8,128)(2,1)} %broadcast_in_dim.225), calls=%async_computation.4 | async-start | bytes 2883584 | tf_op jit(solution)/shard_map/all_to_all | solution.py:131
  76.2 6.4 %copy.88.out_hbm = bf16[1536,1326]{1,0:T(8,128)(2,1)} copy(bf16[1536,1326]{0,1:T(8,128)(2,1)} %param.15) | data formatting | bytes 8146944 | tf_op args[7]
  82.5 8.2 %copy.87.table_hbm = bf16[2048,1326]{1,0:T(8,128)(2,1)} copy(bf16[2048,1326]{0,1:T(8,128)(2,1)} %param.9) | data formatting | bytes 10862592 | tf_op args[1]
  91.1 0.1 stack_reshape.41
  91.2 0.2 fusion.45
  91.5 1.2 reduce-window.30
  92.7 0.2 slice_reduce_fusion
  92.9 0.1 broadcast_add_fusion
  93.2 2.0 %select_reduce_fusion = (s32[32,16]{1,0:T(8,128)S(1)}, s32[32,16]{1,0:T(8,128)S(1)}, s32[32,16]{1,0:T(8,128)S(1)}) fusion(s32[32,512]{1,0:T(8,128)S(1)} %bitcast.76, s32[32,512]{1,0:T(8,128)S(1)} %copy_bitcast_fusion, s32[32,16]{1,0:T(8,128)S(1)} %broadcast_add_fusion.2, s32[32,512]{1,0:T(8,128)S(1)} %fusion.19, s32[32,512]{1,0:T(8,128)S(1)} %bitcast.77, ...), kind=kLoop, calls=%fused_computation.9 | loop fusion | flops 2357760 | bytes 335872 | tf_op jit(solution)/shard_map/reduce_sum | solution.py:26
  95.2 0.1 stack_reshape.47
  95.5 0.2 fusion.43
  95.7 0.1 reshape.474
  95.9 0.9 copy.86.index_ref
  96.7 14.1 %all-to-all-done.4 = bf16[32,16,1326]{2,1,0:T(8,128)(2,1)S(1)} async-done(((bf16[32,16,1326]{2,1,0:T(8,128)(2,1)}), bf16[32,16,1326]{2,1,0:T(8,128)(2,1)S(1)}, u32[]{:S(2)}, u32[]{:S(2)}) %all-to-all-start.4) | async-done | bytes 1357856 | tf_op jit(solution)/shard_map/all_to_all | solution.py:131
  110.8 1.1 copy-done
  111.9 45.7 %shard_map.82 = bf16[3,512,1326]{2,1,0:T(8,128)(2,1)} custom-call(f32[512,9]{1,0:T(8,128)} %copy.86.index_ref, bf16[512,1326]{1,0:T(8,128)(2,1)} %bitcast.69, bf16[2048,1326]{1,0:T(8,128)(2,1)} %copy.87.table_hbm, bf16[1326,1536]{1,0:T(8,128)(2,1)} %in_hbm.1, bf16[1536,1326]{1,0:T(8,128)(2,1)} %copy.88.out_hbm), custom_call_target="tpu_custom_call" | custom-call | tf_op jit(solution)/shard_map/pallas_call | solution.py:113
  157.6 6.3 %copy.89 = bf16[3,512,1326]{1,2,0:T(8,128)(2,1)} copy(bf16[3,512,1326]{2,1,0:T(8,128)(2,1)} %shard_map.82) | data formatting | bytes 8146944 | tf_op jit(solution)/shard_map/pallas_call | solution.py:113
  (58 shorter events, 2.2 us)
Async XLA Ops:
  1.3 14.4 %all-to-all-start.1 = ((s32[32,1,16]{2,1,0:T(1,128)}), s32[32,1,16]{2,1,0:T(1,128)S(1)}, u32[]{:S(2)}, u32[]{:S(2)}) async-start(s32[32,1,16]{2,1,0:T(1,128)} %broadcast_in_dim.201), calls=%async_computation.1 | async-start | bytes 32768 | tf_op jit(solution)/shard_map/all_to_all | solution.py:131
  16.6 18.2 %all-to-all-start = ((s32[32,8,512]{2,1,0:T(8,128)}), s32[32,8,512]{2,1,0:T(8,128)S(1)}, u32[]{:S(2)}, u32[]{:S(2)}) async-start(s32[32,8,512]{2,1,0:T(8,128)} %broadcast_in_dim.196), calls=%async_computation | async-start | bytes 1048576 | tf_op jit(solution)/shard_map/all_to_all | solution.py:131
  35.1 37.0 %copy-start.1 = (bf16[16,1326]{1,0:T(8,128)(2,1)S(1)}, bf16[16,1326]{1,0:T(8,128)(2,1)}, u32[]{:S(2)}) copy-start(bf16[16,1326]{1,0:T(8,128)(2,1)} %param.8) | copy-start | bytes 127300
  41.8 13.5 %all-to-all-start.2 = ((s32[32,3,512]{2,1,0:T(4,128)}), s32[32,3,512]{2,1,0:T(4,128)S(1)}, u32[]{:S(2)}, u32[]{:S(2)}) async-start(s32[32,3,512]{2,1,0:T(4,128)} %broadcast_in_dim.207), calls=%async_computation.2 | async-start | bytes 524288 | tf_op jit(solution)/shard_map/all_to_all | solution.py:131
  73.3 37.5 %all-to-all-start.4 = ((bf16[32,16,1326]{2,1,0:T(8,128)(2,1)}), bf16[32,16,1326]{2,1,0:T(8,128)(2,1)S(1)}, u32[]{:S(2)}, u32[]{:S(2)}) async-start(bf16[32,16,1326]{2,1,0:T(8,128)(2,1)} %broadcast_in_dim.225), calls=%async_computation.4 | async-start | bytes 2883584 | tf_op jit(solution)/shard_map/all_to_all | solution.py:131
  110.8 1.1 copy-start
where the time goes:
time: 165 us; the launch traced here: 164 us
  waiting for transfers between devices  45.9 us (28%)
  Pallas kernels  45.7 us (28%)
  local copies, waits for them, and re-layouts  29.9 us (18%)
  starting transfers between devices  15.7 us (10%)
  other arithmetic  12.9 us (8%)
  blocking collectives  12.8 us (8%)
    all_to_all x4, waiting for transfers between devices, share(): lax.all_to_all(copies, 'owner', split_axis=0, concat_axis=0, tiled=True)  45.9 us
    pallas_call x1, Pallas kernels, rebuild(): pl.pallas_call(rebuild_kernel, grid=(steps,), out_shape=jax.ShapeDtypeStr...  45.7 us
    unnamed x14, local copies, waits for them, and re-layouts  15.7 us
    all_to_all x4, starting transfers between devices, share(): lax.all_to_all(copies, 'owner', split_axis=0, concat_axis=0, tiled=True)  15.7 us
    all_to_all x1, blocking collectives, share(): lax.all_to_all(copies, 'owner', split_axis=0, concat_axis=0, tiled=True)  12.8 us
    reduce_sum x4, other arithmetic, pick(): return jnp.sum(jnp.where(onehot, values[:, None, :], 0), axis=2)  7.89 us
    pallas_call x1, local copies, waits for them, and re-layouts, rebuild(): pl.pallas_call(rebuild_kernel, grid=(steps,), out_shape=jax.ShapeDtypeStr...  6.33 us
    broadcast_in_dim x5, local copies, waits for them, and re-layouts, share(): copies = jnp.broadcast_to(block[None], (devices,) + block.shape)  4.1 us
  transfers between devices with their start and end apart: 4, of which 4 were waited for; matrix products, arithmetic and copies ran while one was open for 13% of the time, Pallas kernels for 0%

commit v1 on v0

v1 whole, which is shorter than its diff:
```python
import functools

import jax
import jax.numpy as jnp
from jax import lax
from jax.experimental import pallas as pl
from jax.experimental.pallas import tpu as pltpu
from jax.sharding import PartitionSpec as P

LEVELS = 3
SLOTS = 512
RECV_DEV = 512
NODE_DEV = 384
CORES = 2
PLANE = 8
HALF = 1 << 16
MESH = pl.DeviceIdType.MESH


def send_slots(owners, devices, capacity):
    slots = owners.shape[0]
    hit = owners[None, :] == jnp.arange(devices, dtype=jnp.int32)[:, None]
    upper = jnp.triu(jnp.ones((slots, slots), jnp.bfloat16))
    count = jnp.dot(hit.astype(jnp.bfloat16), upper, preferred_element_type=jnp.float32).astype(
        jnp.int32
    )
    rank = jnp.where(hit, count - 1, -1)
    return rank[:, None, :] == jnp.arange(capacity, dtype=jnp.int32)[None, :, None]


def pick(onehot, values):
    return jnp.sum(jnp.where(onehot, values[None, None, :], 0), axis=2)


def children_of(counts, slot):
    ends = jnp.cumsum(counts)
    parent = ((ends - counts)[None, None, :] <= slot[:, :, None]) & (
        slot[:, :, None] < ends[None, None, :]
    )
    return parent, jnp.minimum(ends[-1], SLOTS)


def step_place(step):
    level, begin = jnp.int32(0), jnp.int32(0)
    for depth in range(1, LEVELS):
        start = depth * (depth + 1) // 2
        level = jnp.where(step >= start, depth, level)
        begin = jnp.where(step >= start, start, begin)
    return level, step == begin, step == begin + level


def dot_last(left, right):
    return lax.dot_general(
        left, right, (((1,), (1,)), ((), ())), preferred_element_type=jnp.float32
    )


def rebuild_kernel(
    index_ref,
    roots_hbm,
    table_hbm,
    in_hbm,
    out_hbm,
    values_ref,
    roots_ref,
    table_ref,
    in_ref,
    out_ref,
    rows_ref,
    sems,
):
    step = pl.program_id(0)
    level, first, last = step_place(step)
    copies = [
        pltpu.make_async_copy(source, target, sems.at[k])
        for k, (source, target) in enumerate(
            (
                (roots_hbm, roots_ref),
                (table_hbm, table_ref),
                (in_hbm, in_ref),
                (out_hbm, out_ref),
            )
        )
    ]

    @pl.when(step == 0)
    def _():
        for copy in copies:
            copy.start()
        copies[0].wait()
        copies[1].wait()

    index = index_ref[...]
    lane = lax.broadcasted_iota(jnp.int32, index.shape, 1)

    def column(place):
        return jnp.sum(jnp.where(lane == place, index, 0.0), axis=1, keepdims=True)

    def picked(place, entries):
        entry = lax.broadcasted_iota(jnp.int32, (index.shape[0], entries), 1)
        onehot = jnp.where(entry.astype(jnp.float32) == column(place), 1.0, 0.0)
        return onehot.astype(jnp.bfloat16)

    root_place = LEVELS * (LEVELS + 1) // 2 + level

    @pl.when(first)
    def _():
        rows_ref[...] = jnp.dot(
            picked(root_place, roots_ref.shape[0]),
            roots_ref[...],
            preferred_element_type=jnp.float32,
        ).astype(jnp.bfloat16)

    rows = rows_ref[...].astype(jnp.float32) * dot_last(
        picked(step, table_ref.shape[1]), table_ref[...]
    )
    mass = jnp.sum(rows, axis=1, keepdims=True)
    mass = jnp.where(column(root_place) >= 0.0, mass, 1.0)
    rows_ref[...] = (rows * (rows.shape[1] / mass)).astype(jnp.bfloat16)

    @pl.when(step == 0)
    def _():
        copies[2].wait()
        copies[3].wait()

    @pl.when(last)
    def _():
        hidden = jnp.dot(rows_ref[...], in_ref[...], preferred_element_type=jnp.float32)
        hidden = jnp.maximum(hidden, 0.0).astype(jnp.bfloat16)
        values_ref[0] = dot_last(out_ref[...], hidden).astype(jnp.bfloat16)


def rebuild(index, roots, table, value_in, value_out):
    rows, hands = index.shape[0], table.shape[0]
    steps = LEVELS * (LEVELS + 1) // 2
    return pl.pallas_call(
        rebuild_kernel,
        grid=(steps,),
        out_shape=jax.ShapeDtypeStruct((LEVELS, hands, rows), jnp.bfloat16),
        in_specs=[pl.BlockSpec(index.shape, lambda step: (0, 0))]
        + [pl.BlockSpec(memory_space=pl.ANY)] * 4,
        out_specs=pl.BlockSpec((1, hands, rows), lambda step: (step_place(step)[0], 0, 0)),
        scratch_shapes=[
            pltpu.VMEM(array.shape, array.dtype) for array in (roots, table, value_in, value_out)
        ]
        + [pltpu.VMEM((rows, hands), jnp.bfloat16), pltpu.SemaphoreType.DMA((4,))],
        compiler_params=pltpu.CompilerParams(vmem_limit_bytes=56 * 1024 * 1024),
    )(index, roots, table, value_in, value_out)


def place_of(mine):
    return mine // PLANE, mine % PLANE // CORES, mine % CORES


def exchange_kernel(devices, stage, notes_ref, rows_ref, out_notes_ref, out_rows_ref, *sems):
    note_send, note_recv, row_send, row_recv, own_sem = sems
    mine = lax.axis_index("owner")
    line, chip, core = place_of(mine)

    barrier = pltpu.get_barrier_semaphore()

    @pl.loop(1, devices)
    def _(turn):
        peer = lax.rem(mine + turn, devices)
        pl.semaphore_signal(barrier, inc=1, device_id=(peer,), device_id_type=MESH)

    pl.semaphore_wait(barrier, devices - 1)

    def note(turn):
        peer = lax.rem(mine + turn, devices)
        return pltpu.make_async_remote_copy(
            src_ref=notes_ref.at[peer],
            dst_ref=out_notes_ref.at[mine],
            send_sem=note_send.at[turn - 1],
            recv_sem=note_recv.at[turn - 1],
            device_id=(peer,),
            device_id_type=MESH,
        )

    @pl.loop(1, devices)
    def _(turn):
        note(turn).start()

    parts = out_rows_ref.shape[0]
    slot = (line, chip, core)[stage]
    moves = []
    for turn in range(1, parts):
        other = lax.rem(slot + turn, parts)
        peer = (
            other * PLANE + mine % PLANE,
            line * PLANE + other * CORES + core,
            line * PLANE + chip * CORES + other,
        )[stage]
        moves.append(
            pltpu.make_async_remote_copy(
                src_ref=rows_ref,
                dst_ref=out_rows_ref.at[slot],
                send_sem=row_send.at[turn - 1],
                recv_sem=row_recv.at[turn - 1],
                device_id=(peer,),
                device_id_type=MESH,
            )
        )
    for move in moves:
        move.start()
    own = (
        pltpu.make_async_copy(notes_ref.at[mine], out_notes_ref.at[mine], own_sem.at[0]),
        pltpu.make_async_copy(rows_ref, out_rows_ref.at[slot], own_sem.at[1]),
    )
    for copy in own:
        copy.start()

    @pl.loop(1, devices)
    def _(turn):
        note(turn).wait()

    for move in moves:
        move.wait()
    for copy in own:
        copy.wait()


def exchange(stage, notes, rows):
    devices = lax.axis_size("owner")
    parts = (devices // PLANE, PLANE // CORES, CORES)[stage]
    width = -(-notes.shape[1] // 128) * 128
    notes = jnp.pad(notes, ((0, 0), (0, width - notes.shape[1])))[:, None, :]
    out_notes, out_rows = pl.pallas_call(
        functools.partial(exchange_kernel, devices, stage),
        out_shape=(
            jax.ShapeDtypeStruct(notes.shape, notes.dtype),
            jax.ShapeDtypeStruct((parts,) + rows.shape, rows.dtype),
        ),
        in_specs=[pl.BlockSpec(memory_space=pltpu.VMEM)] * 2,
        out_specs=(pl.BlockSpec(memory_space=pltpu.VMEM),) * 2,
        scratch_shapes=[
            pltpu.SemaphoreType.DMA((devices - 1,)),
            pltpu.SemaphoreType.DMA((devices - 1,)),
            pltpu.SemaphoreType.DMA((max(parts - 1, 1),)),
            pltpu.SemaphoreType.DMA((max(parts - 1, 1),)),
            pltpu.SemaphoreType.DMA((2,)),
        ],
        compiler_params=pltpu.CompilerParams(collective_id=stage, has_side_effects=True),
    )(notes, rows)
    return out_notes[:, 0, :], out_rows


def on_device(
    frontier,
    policy_table,
    first_counts,
    policy_index,
    owner_index,
    next_counts,
    value_in,
    value_out,
):
    devices = lax.axis_size("owner")
    mine = lax.axis_index("owner")
    capacity = RECV_DEV // devices
    kept_limit = NODE_DEV * devices
    line, chip, core = place_of(mine)
    lines, chips = devices // PLANE, PLANE // CORES
    first_root = ((core * chips + chip) * lines + line) * frontier.shape[0]
    onehots = [send_slots(owner_index[depth], devices, capacity) for depth in range(LEVELS)]
    slot_index = jnp.arange(SLOTS, dtype=jnp.int32)
    slots = [pick(onehot, slot_index + 1) - 1 for onehot in onehots]
    notes = list(slots)
    for depth in range(LEVELS):
        value = policy_index[depth]
        if depth < LEVELS - 1:
            value = value + HALF * next_counts[depth]
        notes.append(pick(onehots[depth], value))
    lineage = [first_root + jnp.arange(frontier.shape[0], dtype=jnp.int32)]
    counts = first_counts
    rows = frontier
    columns, root_columns = [], []
    for depth in range(LEVELS):
        parent, total = children_of(counts, slots[depth])
        notes += [pick(parent, part) for part in lineage]
        notes.append(jnp.broadcast_to(total, (devices, 1)))
        received, rows = exchange(depth, jnp.concatenate(notes, axis=1), rows)
        if depth == 0:
            first = [
                received[:, k * capacity : (k + 1) * capacity] for k in range(2 * LEVELS)
            ]
            received = received[:, 2 * LEVELS * capacity :]
        lineage = [
            received[:, k * capacity : (k + 1) * capacity] for k in range(len(lineage))
        ]
        totals = received[:, len(lineage) * capacity]
        offsets = jnp.cumsum(totals) - totals
        slot = first[depth]
        policy = first[LEVELS + depth] % HALF
        kept = (slot >= 0) & (slot < totals[:, None]) & (offsets[:, None] + slot < kept_limit)
        if depth == 0:
            path = lineage + [policy]
        elif depth == 1:
            path = [lineage[0] % HALF, lineage[0] // HALF, policy]
        else:
            path = [lineage[0] % HALF, lineage[0] // HALF, lineage[1], policy]
        root_columns.append(jnp.where(kept, path[0], -1))
        columns += path[1:]
        counts = jnp.where(kept, first[LEVELS + depth] // HALF, 0).reshape(-1)
        path = [part.reshape(-1) for part in path]
        lineage = [path[0] + HALF * path[1]] + path[2:]
        notes = []
    roots = rows.reshape(-1, rows.shape[-1])
    index = jnp.stack([part.reshape(-1) for part in columns + root_columns], axis=1)
    values = rebuild(
        index.astype(jnp.float32), roots, policy_table.T, value_in, value_out.T
    )
    return jnp.swapaxes(values, 1, 2)


def solution(mesh):
    placed = (
        P("owner", None),
        P(),
        P("owner"),
        P(None, "owner"),
        P(None, "owner"),
        P(None, "owner"),
        P(),
        P(),
    )
    return jax.shard_map(
        on_device, mesh=mesh, in_specs=placed, out_specs=P(None, "owner", None), check_vma=False
    )
```

time: 165 us -> 118 us (0.72)
  waiting for transfers between devices: 45.9 us -> 0 us
  Pallas kernels: 45.7 us -> 85.1 us
  local copies, waits for them, and re-layouts: 29.9 us -> 9.72 us
  starting transfers between devices: 15.7 us -> 0 us
  blocking collectives: 12.8 us -> 0 us
  other arithmetic: 12.9 us -> 17.4 us
  between operations: 0.36 us -> 2.27 us
    all_to_all x4 -> x0, waiting for transfers between devices: 45.9 us -> none  [share(): lax.all_to_all(copies, 'owner', split_axis=0, concat_axis=0, tiled=True)]
    pallas_call x0 -> x3, Pallas kernels: none -> 40.5 us  [exchange(): pl.pallas_call(functools.partial(exchange_kernel, devices, stage), out_sh...]
    unnamed x14 -> x0, local copies, waits for them, and re-layouts: 15.7 us -> none
    all_to_all x4 -> x0, starting transfers between devices: 15.7 us -> none  [share(): lax.all_to_all(copies, 'owner', split_axis=0, concat_axis=0, tiled=True)]
    all_to_all x1 -> x0, blocking collectives: 12.8 us -> none  [share(): lax.all_to_all(copies, 'owner', split_axis=0, concat_axis=0, tiled=True)]
    pallas_call x1 -> x0, local copies, waits for them, and re-layouts: 6.33 us -> none  [rebuild(): pl.pallas_call(rebuild_kernel, grid=(steps,), out_shape=jax.ShapeDtypeStr...]
    select_n x3 -> x5, other arithmetic: 0.23 us -> 4.3 us  [the longest x2 1.8 us: on_device(): counts = jnp.where(kept, first[LEVELS + depth] // HALF, 0).reshape(-1)]
    slice x4 -> x8, local copies, waits for them, and re-layouts: 0.9 us -> 4.96 us  [the longest x3 2.37 us: on_device(): totals = received[:, len(lineage) * capacity]]
  transfers between devices with their start and end apart: 4 -> 0, of which waited for: 4 -> 0; matrix products, arithmetic and copies ran while one was open for 13% -> 0% of each run, Pallas kernels for 0% -> 0%
where the time goes in v1:
time: 118 us; the launch traced here: 115 us
  Pallas kernels  85.1 us (72%)
  other arithmetic  17.4 us (15%)
  local copies, waits for them, and re-layouts  9.72 us (8%)
  between operations  2.27 us (2%)
    pallas_call x1, Pallas kernels, rebuild(): pl.pallas_call(rebuild_kernel, grid=(steps,), out_shape=jax.ShapeDtypeStr...  44.6 us
    pallas_call x3, Pallas kernels, exchange(): pl.pallas_call(functools.partial(exchange_kernel, devices, stage), out_sh...  40.5 us
    reduce_sum x4, other arithmetic, pick(): return jnp.sum(jnp.where(onehot, values[None, None, :], 0), axis=2)  5.46 us
    slice x3, other arithmetic, on_device(): totals = received[:, len(lineage) * capacity]  2.69 us
    slice x3, local copies, waits for them, and re-layouts, on_device(): totals = received[:, len(lineage) * capacity]  2.37 us

profile of v1, /device:TPU:0, one launch (start us, length us, event | category | flops | bytes accessed | tf_op | source)
XLA Modules:
  0.0 115.4 jit_solution(12298492965131198943)
XLA Ops:
  0.0 0.8 multiply_add_fusion.2
  0.8 0.8 fusion.45
  1.7 0.7 copy.30
  2.4 0.5 slice.118
  3.6 0.1 reduce
  3.7 0.7 sub.78
  4.4 0.3 fusion.5
  4.6 0.3 fusion.1
  4.9 0.3 fusion.3
  5.2 3.4 %select_reduce_fusion.3 = (s32[32,16]{1,0:T(8,128)S(1)}, s32[32,16]{1,0:T(8,128)S(1)}, s32[32,16]{1,0:T(8,128)S(1)}, s32[32,16]{1,0:T(8,128)S(1)}, s32[32,16]{1,0:T(8,128)S(1)}, /*index=5*/s32[32,16]{1,0:T(8,128)S(1)}) fusion(s32[512]{0:T(512)S(1)} %bitcast.51, s32[32,512]{1,0:T(8,128)S(1)} %fusion.1, s32[512]{0:T(512)S(1)} %iota_add_fusion, ...), kind=kLoop, calls=%fused_computation.12 | loop fusion | flops 3929088 | bytes 217088 | tf_op jit(solution)/shard_map/reduce_sum | solution.py:32
  8.6 0.1 select_reduce_fusion.9
  8.8 0.1 concatenate.9
  8.9 0.6 pad.13
  9.6 14.1 %shard_map.82 = (s32[32,1,128]{2,1,0:T(1,128)}, bf16[4,16,1326]{2,1,0:T(8,128)(2,1)}) custom-call(s32[32,1,128]{2,1,0:T(1,128)} %bitcast.48, bf16[16,1326]{1,0:T(8,128)(2,1)} %rows_ref.1), custom_call_target="tpu_custom_call" | custom-call | tf_op jit(solution)/shard_map/pallas_call | solution.py:228
  23.6 0.8 slice.121
  24.5 0.9 slice_reduce_fusion.4
  25.4 0.9 fusion.22
  26.3 0.1 stack_reshape.33
  26.5 0.3 reduce-window.34
  27.0 0.1 slice_reduce_fusion.1
  27.2 0.6 slice.105
  28.4 0.9 multiply_add_fusion.1
  29.4 0.7 select_reduce_fusion.2
  30.1 0.6 pad_select_fusion
  30.8 16.1 %shard_map.83 = (s32[32,1,128]{2,1,0:T(1,128)}, bf16[4,4,16,1326]{3,2,1,0:T(8,128)(2,1)}) custom-call(s32[32,1,128]{2,1,0:T(1,128)} %bitcast.46, bf16[4,16,1326]{2,1,0:T(8,128)(2,1)} %get-tuple-element.12.rows_ref), custom_call_target="tpu_custom_call" | custom-call | tf_op jit(solution)/shard_map/pallas_call | solution.py:228
  46.9 0.8 slice.126
  47.7 0.9 slice_reduce_fusion.3
  48.6 0.9 fusion.23
  49.5 0.1 stack_reshape.34
  49.8 0.3 reduce-window.39
  50.2 0.1 slice_reduce_fusion
  50.4 0.6 slice.112
  51.7 0.7 multiply_add_fusion
  52.4 0.1 add.202
  52.6 0.9 add_select_fusion.1
  53.5 0.1 stack_reshape.32
  53.7 1.3 %select_reduce_fusion.1 = (s32[32,16]{1,0:T(8,128)S(1)}, s32[32,16]{1,0:T(8,128)S(1)}) fusion(s32[512]{0:T(512)S(1)} %add.202, s32[512]{0:T(512)S(1)} %get-tuple-element.36, s32[32,16]{1,0:T(8,128)S(1)} %get-tuple-element.63, s32[512]{0:T(512)S(1)} %get-tuple-element.35, s32[512]{0:T(512)S(1)} %broadcast_in_dim.154), kind=kLoop, calls=%fused_computation.10 | loop fusion | flops 1833984 | bytes 14336 | tf_op jit(solution)/shard_map/reduce_sum | solution.py:32
  55.1 0.6 pad.15
  55.7 10.3 %shard_map.84 = (s32[32,1,128]{2,1,0:T(1,128)}, bf16[2,4,4,16,1326]{4,3,2,1,0:T(8,128)(2,1)}) custom-call(s32[32,1,128]{2,1,0:T(1,128)} %bitcast.47, bf16[4,4,16,1326]{3,2,1,0:T(8,128)(2,1)} %get-tuple-element.14.rows_ref), custom_call_target="tpu_custom_call" | custom-call | tf_op jit(solution)/shard_map/pallas_call | solution.py:228
  66.1 0.8 slice.131
  66.9 0.9 slice_reduce_fusion.2
  67.8 0.9 fusion.25
  68.7 0.1 stack_reshape.35
  68.8 0.7 add_select_fusion.2
  69.5 0.1 stack_reshape.30
  69.6 0.1 stack_reshape.31
  69.7 0.8 copy.34.index_ref
  70.6 44.6 %shard_map.85 = bf16[3,1326,512]{2,1,0:T(8,128)(2,1)} custom-call(f32[512,9]{1,0:T(8,128)} %copy.34.index_ref, bf16[512,1326]{1,0:T(8,128)(2,1)} %bitcast.37, bf16[1326,2048]{1,0:T(8,128)(2,1)} %bitcast.28, bf16[1326,1536]{1,0:T(8,128)(2,1)} %in_hbm.1, bf16[1326,1536]{1,0:T(8,128)(2,1)} %bitcast.29), custom_call_target="tpu_custom_call" | custom-call | tf_op jit(solution)/shard_map/pallas_call | solution.py:136
  (31 shorter events, 1.7 us)

commit v2 on v1

--- a/solution.py
+++ b/solution.py
@@ -55,8 +55,20 @@
     )
 
 
+def column_of(index, place):
+    lane = lax.broadcasted_iota(jnp.int32, index.shape, 1)
+    return jnp.sum(jnp.where(lane == place, index, 0.0), axis=1, keepdims=True)
+
+
+def picked(index, place, entries):
+    entry = lax.broadcasted_iota(jnp.int32, (index.shape[0], entries), 1)
+    onehot = jnp.where(entry.astype(jnp.float32) == column_of(index, place), 1.0, 0.0)
+    return onehot.astype(jnp.bfloat16)
+
+
 def rebuild_kernel(
     index_ref,
+    policy_ref,
     roots_hbm,
     table_hbm,
     in_hbm,
@@ -67,6 +79,7 @@
     in_ref,
     out_ref,
     rows_ref,
+    factor_ref,
     sems,
 ):
     step = pl.program_id(0)
@@ -76,9 +89,9 @@
         for k, (source, target) in enumerate(
             (
                 (roots_hbm, roots_ref),
-                (table_hbm, table_ref),
                 (in_hbm, in_ref),
                 (out_hbm, out_ref),
+                (table_hbm, table_ref),
             )
         )
     ]
@@ -88,40 +101,40 @@
         for copy in copies:
             copy.start()
         copies[0].wait()
-        copies[1].wait()
+
+    @pl.when(step == 1)
+    def _():
+        copies[3].wait()
 
     index = index_ref[...]
-    lane = lax.broadcasted_iota(jnp.int32, index.shape, 1)
-
-    def column(place):
-        return jnp.sum(jnp.where(lane == place, index, 0.0), axis=1, keepdims=True)
-
-    def picked(place, entries):
-        entry = lax.broadcasted_iota(jnp.int32, (index.shape[0], entries), 1)
-        onehot = jnp.where(entry.astype(jnp.float32) == column(place), 1.0, 0.0)
-        return onehot.astype(jnp.bfloat16)
-
     root_place = LEVELS * (LEVELS + 1) // 2 + level
 
     @pl.when(first)
     def _():
         rows_ref[...] = jnp.dot(
-            picked(root_place, roots_ref.shape[0]),
+            picked(index, root_place, roots_ref.shape[0]),
             roots_ref[...],
             preferred_element_type=jnp.float32,
         ).astype(jnp.bfloat16)
 
-    rows = rows_ref[...].astype(jnp.float32) * dot_last(
-        picked(step, table_ref.shape[1]), table_ref[...]
-    )
+    @pl.when(last)
+    def _():
+        factor_ref[...] = policy_ref[0]
+
+    @pl.when(jnp.logical_not(last))
+    def _():
+        factor = dot_last(picked(index, step, table_ref.shape[1]), table_ref[...])
+        factor_ref[...] = factor.astype(jnp.bfloat16)
+
+    rows = rows_ref[...].astype(jnp.float32) * factor_ref[...].astype(jnp.float32)
     mass = jnp.sum(rows, axis=1, keepdims=True)
-    mass = jnp.where(column(root_place) >= 0.0, mass, 1.0)
+    mass = jnp.where(column_of(index, root_place) >= 0.0, mass, 1.0)
     rows_ref[...] = (rows * (rows.shape[1] / mass)).astype(jnp.bfloat16)
 
     @pl.when(step == 0)
     def _():
+        copies[1].wait()
         copies[2].wait()
-        copies[3].wait()
 
     @pl.when(last)
     def _():
@@ -130,30 +143,42 @@
         values_ref[0] = dot_last(out_ref[...], hidden).astype(jnp.bfloat16)
 
 
-def rebuild(index, roots, table, value_in, value_out):
+def rebuild(index, policy_rows, roots, table, value_in, value_out):
     rows, hands = index.shape[0], table.shape[0]
     steps = LEVELS * (LEVELS + 1) // 2
     return pl.pallas_call(
         rebuild_kernel,
         grid=(steps,),
         out_shape=jax.ShapeDtypeStruct((LEVELS, hands, rows), jnp.bfloat16),
-        in_specs=[pl.BlockSpec(index.shape, lambda step: (0, 0))]
+        in_specs=[
+            pl.BlockSpec(index.shape, lambda step: (0, 0)),
+            pl.BlockSpec((1, rows, hands), lambda step: (step_place(step)[0], 0, 0)),
+        ]
         + [pl.BlockSpec(memory_space=pl.ANY)] * 4,
         out_specs=pl.BlockSpec((1, hands, rows), lambda step: (step_place(step)[0], 0, 0)),
         scratch_shapes=[
             pltpu.VMEM(array.shape, array.dtype) for array in (roots, table, value_in, value_out)
         ]
-        + [pltpu.VMEM((rows, hands), jnp.bfloat16), pltpu.SemaphoreType.DMA((4,))],
+        + [pltpu.VMEM((rows, hands), jnp.bfloat16)] * 2
+        + [pltpu.SemaphoreType.DMA((4,))],
         compiler_params=pltpu.CompilerParams(vmem_limit_bytes=56 * 1024 * 1024),
-    )(index, roots, table, value_in, value_out)
+    )(index, policy_rows, roots, table, value_in, value_out)
 
 
 def place_of(mine):
     return mine // PLANE, mine % PLANE // CORES, mine % CORES
 
 
-def exchange_kernel(devices, stage, notes_ref, rows_ref, out_notes_ref, out_rows_ref, *sems):
-    note_send, note_recv, row_send, row_recv, own_sem = sems
+def exchange_kernel(devices, stage, *refs):
+    if len(refs) == 9:
+        notes_ref, rows_ref, out_notes_ref, out_rows_ref = refs[:4]
+    else:
+        notes_ref, rows_ref, index_ref, table_hbm, out_notes_ref, out_rows_ref, policy_hbm = refs[:7]
+        table_ref, policy_ref, policy_sem = refs[12:]
+        refs = refs[3:12]
+        load = pltpu.make_async_copy(table_hbm, table_ref, policy_sem.at[LEVELS])
+        load.start()
+    note_send, note_recv, row_send, row_recv, own_sem = refs[4:9]
     mine = lax.axis_index("owner")
     line, chip, core = place_of(mine)
 
@@ -210,6 +235,23 @@
     for copy in own:
         copy.start()
 
+    if stage == 1:
+        load.wait()
+
+        def store(depth):
+            return pltpu.make_async_copy(
+                policy_ref.at[depth], policy_hbm.at[depth], policy_sem.at[depth]
+            )
+
+        @pl.loop(0, LEVELS)
+        def _(depth):
+            onehot = picked(index_ref[...], depth, table_ref.shape[1])
+            policy_ref[depth] = dot_last(onehot, table_ref[...]).astype(jnp.bfloat16)
+            store(depth).start()
+
+        for depth in range(LEVELS):
+            store(depth).wait()
+
     @pl.loop(1, devices)
     def _(turn):
         note(turn).wait()
@@ -220,29 +262,46 @@
         copy.wait()
 
 
-def exchange(stage, notes, rows):
+def exchange(stage, notes, rows, extra=()):
     devices = lax.axis_size("owner")
     parts = (devices // PLANE, PLANE // CORES, CORES)[stage]
     width = -(-notes.shape[1] // 128) * 128
     notes = jnp.pad(notes, ((0, 0), (0, width - notes.shape[1])))[:, None, :]
-    out_notes, out_rows = pl.pallas_call(
+    vmem, anywhere = pl.BlockSpec(memory_space=pltpu.VMEM), pl.BlockSpec(memory_space=pl.ANY)
+    out_shape = [
+        jax.ShapeDtypeStruct(notes.shape, notes.dtype),
+        jax.ShapeDtypeStruct((parts,) + rows.shape, rows.dtype),
+    ]
+    in_specs, out_specs = [vmem, vmem], [vmem, vmem]
+    scratch = [
+        pltpu.SemaphoreType.DMA((devices - 1,)),
+        pltpu.SemaphoreType.DMA((devices - 1,)),
+        pltpu.SemaphoreType.DMA((max(parts - 1, 1),)),
+        pltpu.SemaphoreType.DMA((max(parts - 1, 1),)),
+        pltpu.SemaphoreType.DMA((2,)),
+    ]
+    if extra:
+        index, table = extra
+        shape = (LEVELS, index.shape[0], table.shape[0])
+        out_shape.append(jax.ShapeDtypeStruct(shape, table.dtype))
+        in_specs += [vmem, anywhere]
+        out_specs.append(anywhere)
+        scratch += [
+            pltpu.VMEM(table.shape, table.dtype),
+            pltpu.VMEM(shape, table.dtype),
+            pltpu.SemaphoreType.DMA((LEVELS + 1,)),
+        ]
+    out = pl.pallas_call(
         functools.partial(exchange_kernel, devices, stage),
-        out_shape=(
-            jax.ShapeDtypeStruct(notes.shape, notes.dtype),
-            jax.ShapeDtypeStruct((parts,) + rows.shape, rows.dtype),
+        out_shape=out_shape,
+        in_specs=in_specs,
+        out_specs=out_specs,
+        scratch_shapes=scratch,
+        compiler_params=pltpu.CompilerParams(
+            collective_id=stage, has_side_effects=True, vmem_limit_bytes=48 * 1024 * 1024
         ),
-        in_specs=[pl.BlockSpec(memory_space=pltpu.VMEM)] * 2,
-        out_specs=(pl.BlockSpec(memory_space=pltpu.VMEM),) * 2,
-        scratch_shapes=[
-            pltpu.SemaphoreType.DMA((devices - 1,)),
-            pltpu.SemaphoreType.DMA((devices - 1,)),
-            pltpu.SemaphoreType.DMA((max(parts - 1, 1),)),
-            pltpu.SemaphoreType.DMA((max(parts - 1, 1),)),
-            pltpu.SemaphoreType.DMA((2,)),
-        ],
-        compiler_params=pltpu.CompilerParams(collective_id=stage, has_side_effects=True),
-    )(notes, rows)
-    return out_notes[:, 0, :], out_rows
+    )(notes, rows, *extra)
+    return (out[0][:, 0, :],) + tuple(out[1:])
 
 
 def on_device(
@@ -279,7 +338,16 @@
         parent, total = children_of(counts, slots[depth])
         notes += [pick(parent, part) for part in lineage]
         notes.append(jnp.broadcast_to(total, (devices, 1)))
-        received, rows = exchange(depth, jnp.concatenate(notes, axis=1), rows)
+        notes = jnp.concatenate(notes, axis=1)
+        if depth == 1:
+            last_index = jnp.stack(
+                [(part % HALF).reshape(-1) for part in first[LEVELS:]], axis=1
+            ).astype(jnp.float32)
+            received, rows, policy_rows = exchange(
+                depth, notes, rows, (last_index, policy_table.T)
+            )
+        else:
+            received, rows = exchange(depth, notes, rows)
         if depth == 0:
             first = [
                 received[:, k * capacity : (k + 1) * capacity] for k in range(2 * LEVELS)
@@ -308,7 +376,7 @@
     roots = rows.reshape(-1, rows.shape[-1])
     index = jnp.stack([part.reshape(-1) for part in columns + root_columns], axis=1)
     values = rebuild(
-        index.astype(jnp.float32), roots, policy_table.T, value_in, value_out.T
+        index.astype(jnp.float32), policy_rows, roots, policy_table.T, value_in, value_out.T
     )
     return jnp.swapaxes(values, 1, 2)
 

time: 118 us -> 96.4 us (0.82); the launches traced: 115 us -> 96 us
  Pallas kernels: 85.1 us -> 73.3 us
  other arithmetic: 17.4 us -> 9.18 us
    pallas_call x1, Pallas kernels: 44.6 us -> 36.7 us  [rebuild(): pl.pallas_call(rebuild_kernel, grid=(steps,), out_shape=jax.ShapeDtypeStr...]
    unnamed x0 -> x6, local copies, waits for them, and re-layouts: none -> 3.88 us
    pallas_call x3, Pallas kernels: 40.5 us -> 36.7 us  [exchange(): pl.pallas_call(functools.partial(exchange_kernel, devices, stage), out_sh...]
    select_n x3 -> x1, other arithmetic: 2.68 us -> 0.1 us  [on_device(): part % HALF]
    slice x3, local copies, waits for them, and re-layouts: 2.37 us -> 0.22 us  [on_device(): totals = received[:, len(lineage) * capacity]]
    slice x3, other arithmetic: 2.69 us -> 0.55 us  [on_device(): totals = received[:, len(lineage) * capacity]]
    add x2, other arithmetic: 1.61 us -> 0.1 us  [on_device(): lineage = [path[0] + HALF * path[1]] + path[2:]]
    pad x2, local copies, waits for them, and re-layouts: 1.24 us -> 0.01 us  [exchange(): notes = jnp.pad(notes, ((0, 0), (0, width - notes.shape[1])))[:, None, :]]
where the time goes in v2:
time: 96.4 us; the launch traced here: 96 us
  Pallas kernels  73.3 us (76%)
  local copies, waits for them, and re-layouts  10.4 us (11%)
  other arithmetic  9.18 us (10%)
  between operations  2.32 us (2%)
    pallas_call x3, Pallas kernels, exchange(): pl.pallas_call(functools.partial(exchange_kernel, devices, stage), out_sh...  36.7 us
    pallas_call x1, Pallas kernels, rebuild(): pl.pallas_call(rebuild_kernel, grid=(steps,), out_shape=jax.ShapeDtypeStr...  36.7 us
    reduce_sum x4, other arithmetic, pick(): return jnp.sum(jnp.where(onehot, values[None, None, :], 0), axis=2)  5.46 us
    unnamed x6, local copies, waits for them, and re-layouts  3.88 us

profile of v2, /device:TPU:0, one launch (start us, length us, event | category | flops | bytes accessed | tf_op | source)
XLA Modules:
  0.0 96.0 jit_solution(16543072749140018630)
XLA Ops:
  0.0 0.8 multiply_add_fusion.2
  0.8 0.8 fusion.45
  1.7 0.7 copy.35
  2.4 0.5 slice.118
  3.6 0.1 reduce
  3.7 0.7 sub.78
  4.4 0.3 fusion.5
  4.6 0.3 fusion.1
  4.9 0.3 fusion.3
  5.2 3.4 %select_reduce_fusion.3 = (s32[32,16]{1,0:T(8,128)S(1)}, s32[32,16]{1,0:T(8,128)S(1)}, s32[32,16]{1,0:T(8,128)S(1)}, s32[32,16]{1,0:T(8,128)S(1)}, s32[32,16]{1,0:T(8,128)S(1)}, /*index=5*/s32[32,16]{1,0:T(8,128)S(1)}) fusion(s32[512]{0:T(512)S(1)} %bitcast.51, s32[32,512]{1,0:T(8,128)S(1)} %fusion.1, s32[512]{0:T(512)S(1)} %iota_add_fusion, ...), kind=kLoop, calls=%fused_computation.12 | loop fusion | flops 3929088 | bytes 217088 | tf_op jit(solution)/shard_map/reduce_sum | solution.py:32
  8.6 0.1 select_reduce_fusion.9
  8.8 0.1 concatenate.9
  9.0 0.8 copy-done.2
  9.7 12.6 %shard_map.82 = (s32[32,1,128]{2,1,0:T(1,128)S(1)}, bf16[4,16,1326]{2,1,0:T(8,128)(2,1)S(1)}) custom-call(s32[32,1,128]{2,1,0:T(1,128)S(1)} %bitcast.45, bf16[16,1326]{1,0:T(8,128)(2,1)S(1)} %copy-done.2), custom_call_target="tpu_custom_call" | custom-call | tf_op jit(solution)/shard_map/pallas_call | solution.py:294
  22.5 0.2 slice_reduce_fusion.4
  22.7 0.1 add_select_fusion.6
  22.8 0.1 stack_reshape.32
  22.9 0.1 stack_reshape.31
  23.0 0.1 stack_reshape.36
  23.1 0.1 reshape.193
  23.2 0.1 reshape.191
  23.3 0.3 reduce-window.34
  23.7 0.1 slice_reduce_fusion.1
  23.9 0.6 slice.105
  25.1 0.1 multiply_add_fusion.1
  25.2 0.1 add.201
  25.3 0.7 select_reduce_fusion.2
  26.0 0.1 stack_reshape.30
  26.1 0.1 copy.39.refs_2_
  26.3 15.8 %shard_map.83 = (s32[32,1,128]{2,1,0:T(1,128)S(1)}, bf16[4,4,16,1326]{3,2,1,0:T(8,128)(2,1)S(1)}, bf16[3,512,1326]{2,1,0:T(8,128)(2,1)S(1)}) custom-call(s32[32,1,128]{2,1,0:T(1,128)S(1)} %bitcast.43, bf16[4,16,1326]{2,1,0:T(8,128)(2,1)S(1)} %get-tuple-element.13.refs_1_, f32[512,3]{1,0:T(8,128)S(1)} %copy.39.refs_2_, bf16[1326,2048]{1,0:T(8,128)(2,1)} %bitcast.46), custom_call_target="tpu_custom_call" | custom-call | tf_op jit(solution)/shard_map/pallas_call | solution.py:294
  42.1 2.0 %copy-done = bf16[3,512,1326]{2,1,0:T(8,128)(2,1)} copy-done((bf16[3,512,1326]{2,1,0:T(8,128)(2,1)}, bf16[3,512,1326]{2,1,0:T(8,128)(2,1)S(1)}, u32[]{:S(2)}) %copy-start) | copy-done | bytes 4073496
  44.2 0.2 slice_reduce_fusion.3
  44.4 0.1 fusion.33
  44.5 0.1 stack_reshape.37
  44.7 0.3 reduce-window.39
  45.1 0.1 slice_reduce_fusion
  45.3 0.6 slice.113
  46.7 0.1 add.209
  46.7 0.1 stack_reshape.33
  46.8 1.3 %select_reduce_fusion.1 = (s32[32,16]{1,0:T(8,128)S(1)}, s32[32,16]{1,0:T(8,128)S(1)}) fusion(s32[512]{0:T(512)S(1)} %add.209, s32[512]{0:T(512)S(1)} %get-tuple-element.38, s32[32,16]{1,0:T(8,128)S(1)} %get-tuple-element.66, s32[512]{0:T(512)S(1)} %get-tuple-element.37, s32[512]{0:T(512)S(1)} %broadcast_in_dim.154), kind=kLoop, calls=%fused_computation.10 | loop fusion | flops 1833984 | bytes 14336 | tf_op jit(solution)/shard_map/reduce_sum | solution.py:32
  48.2 8.3 %shard_map.84 = (s32[32,1,128]{2,1,0:T(1,128)S(1)}, bf16[2,4,4,16,1326]{4,3,2,1,0:T(8,128)(2,1)S(1)}) custom-call(s32[32,1,128]{2,1,0:T(1,128)S(1)} %bitcast.44, bf16[4,4,16,1326]{3,2,1,0:T(8,128)(2,1)S(1)} %get-tuple-element.15.refs_1_), custom_call_target="tpu_custom_call" | custom-call | tf_op jit(solution)/shard_map/pallas_call | solution.py:294
  56.5 1.1 %copy-done.1 = bf16[2,4,4,16,1326]{4,3,2,1,0:T(8,128)(2,1)} copy-done((bf16[2,4,4,16,1326]{4,3,2,1,0:T(8,128)(2,1)}, bf16[2,4,4,16,1326]{4,3,2,1,0:T(8,128)(2,1)S(1)}, u32[]{:S(2)}) %copy-start.1) | copy-done | bytes 1357848
  57.7 0.2 slice_reduce_fusion.2
  57.9 0.1 fusion.25
  58.0 0.1 stack_reshape.38
  58.1 0.1 stack_reshape.34
  58.3 0.9 copy.40.index_ref
  59.2 36.7 %shard_map.85 = bf16[3,1326,512]{2,1,0:T(8,128)(2,1)} custom-call(f32[512,9]{1,0:T(8,128)} %copy.40.index_ref, bf16[3,512,1326]{2,1,0:T(8,128)(2,1)} %copy-done, bf16[512,1326]{1,0:T(8,128)(2,1)} %bitcast.34, bf16[1326,2048]{1,0:T(8,128)(2,1)} %bitcast.47, bf16[1326,1536]{1,0:T(8,128)(2,1)} %in_hbm.1, bf16[1326,1536]{1,0:T(8,128)(2,1)} %bitcast.48), custom_call_target="tpu_custom_call" | custom-call | tf_op jit(solution)/shard_map/pallas_call | solution.py:149
  (38 shorter events, 1.6 us)
Async XLA Ops:
  9.0 0.8 copy-start.2
  42.1 2.0 %copy-start = (bf16[3,512,1326]{2,1,0:T(8,128)(2,1)}, bf16[3,512,1326]{2,1,0:T(8,128)(2,1)S(1)}, u32[]{:S(2)}) copy-start(bf16[3,512,1326]{2,1,0:T(8,128)(2,1)S(1)} %get-tuple-element.17.policy_ref) | copy-start | bytes 12220420
  56.5 1.1 %copy-start.1 = (bf16[2,4,4,16,1326]{4,3,2,1,0:T(8,128)(2,1)}, bf16[2,4,4,16,1326]{4,3,2,1,0:T(8,128)(2,1)S(1)}, u32[]{:S(2)}) copy-start(bf16[2,4,4,16,1326]{4,3,2,1,0:T(8,128)(2,1)S(1)} %get-tuple-element.18) | copy-start | bytes 4073476

commit v3 on v2

--- a/solution.py
+++ b/solution.py
@@ -69,6 +69,7 @@
 def rebuild_kernel(
     index_ref,
     policy_ref,
+    second_ref,
     roots_hbm,
     table_hbm,
     in_hbm,
@@ -102,7 +103,7 @@
             copy.start()
         copies[0].wait()
 
-    @pl.when(step == 1)
+    @pl.when(step == 3)
     def _():
         copies[3].wait()
 
@@ -121,7 +122,11 @@
     def _():
         factor_ref[...] = policy_ref[0]
 
-    @pl.when(jnp.logical_not(last))
+    @pl.when(step == 1)
+    def _():
+        factor_ref[...] = second_ref[0]
+
+    @pl.when(jnp.logical_not(last) & (step > 1))
     def _():
         factor = dot_last(picked(index, step, table_ref.shape[1]), table_ref[...])
         factor_ref[...] = factor.astype(jnp.bfloat16)
@@ -143,7 +148,7 @@
         values_ref[0] = dot_last(out_ref[...], hidden).astype(jnp.bfloat16)
 
 
-def rebuild(index, policy_rows, roots, table, value_in, value_out):
+def rebuild(index, policy_rows, second_rows, roots, table, value_in, value_out):
     rows, hands = index.shape[0], table.shape[0]
     steps = LEVELS * (LEVELS + 1) // 2
     return pl.pallas_call(
@@ -153,6 +158,7 @@
         in_specs=[
             pl.BlockSpec(index.shape, lambda step: (0, 0)),
             pl.BlockSpec((1, rows, hands), lambda step: (step_place(step)[0], 0, 0)),
+            pl.BlockSpec((1, rows, hands), lambda step: (0, 0, 0)),
         ]
         + [pl.BlockSpec(memory_space=pl.ANY)] * 4,
         out_specs=pl.BlockSpec((1, hands, rows), lambda step: (step_place(step)[0], 0, 0)),
@@ -162,7 +168,7 @@
         + [pltpu.VMEM((rows, hands), jnp.bfloat16)] * 2
         + [pltpu.SemaphoreType.DMA((4,))],
         compiler_params=pltpu.CompilerParams(vmem_limit_bytes=56 * 1024 * 1024),
-    )(index, policy_rows, roots, table, value_in, value_out)
+    )(index, policy_rows, second_rows, roots, table, value_in, value_out)
 
 
 def place_of(mine):
@@ -176,7 +182,7 @@
         notes_ref, rows_ref, index_ref, table_hbm, out_notes_ref, out_rows_ref, policy_hbm = refs[:7]
         table_ref, policy_ref, policy_sem = refs[12:]
         refs = refs[3:12]
-        load = pltpu.make_async_copy(table_hbm, table_ref, policy_sem.at[LEVELS])
+        load = pltpu.make_async_copy(table_hbm, table_ref, policy_sem.at[policy_ref.shape[0]])
         load.start()
     note_send, note_recv, row_send, row_recv, own_sem = refs[4:9]
     mine = lax.axis_index("owner")
@@ -235,7 +241,8 @@
     for copy in own:
         copy.start()
 
-    if stage == 1:
+    if stage > 0:
+        picks = policy_ref.shape[0]
         load.wait()
 
         def store(depth):
@@ -243,13 +250,13 @@
                 policy_ref.at[depth], policy_hbm.at[depth], policy_sem.at[depth]
             )
 
-        @pl.loop(0, LEVELS)
+        @pl.loop(0, picks)
         def _(depth):
             onehot = picked(index_ref[...], depth, table_ref.shape[1])
             policy_ref[depth] = dot_last(onehot, table_ref[...]).astype(jnp.bfloat16)
             store(depth).start()
 
-        for depth in range(LEVELS):
+        for depth in range(picks):
             store(depth).wait()
 
     @pl.loop(1, devices)
@@ -282,14 +289,14 @@
     ]
     if extra:
         index, table = extra
-        shape = (LEVELS, index.shape[0], table.shape[0])
+        shape = (index.shape[1], index.shape[0], table.shape[0])
         out_shape.append(jax.ShapeDtypeStruct(shape, table.dtype))
         in_specs += [vmem, anywhere]
         out_specs.append(anywhere)
         scratch += [
             pltpu.VMEM(table.shape, table.dtype),
             pltpu.VMEM(shape, table.dtype),
-            pltpu.SemaphoreType.DMA((LEVELS + 1,)),
+            pltpu.SemaphoreType.DMA((index.shape[1] + 1,)),
         ]
     out = pl.pallas_call(
         functools.partial(exchange_kernel, devices, stage),
@@ -333,26 +340,24 @@
     lineage = [first_root + jnp.arange(frontier.shape[0], dtype=jnp.int32)]
     counts = first_counts
     rows = frontier
-    columns, root_columns = [], []
+    columns, root_columns, policy_rows = [], [], []
     for depth in range(LEVELS):
         parent, total = children_of(counts, slots[depth])
         notes += [pick(parent, part) for part in lineage]
         notes.append(jnp.broadcast_to(total, (devices, 1)))
         notes = jnp.concatenate(notes, axis=1)
-        if depth == 1:
-            last_index = jnp.stack(
-                [(part % HALF).reshape(-1) for part in first[LEVELS:]], axis=1
-            ).astype(jnp.float32)
-            received, rows, policy_rows = exchange(
-                depth, notes, rows, (last_index, policy_table.T)
-            )
+        if depth == 0:
+            received, rows = exchange(depth, notes, rows)
         else:
-            received, rows = exchange(depth, notes, rows)
+            wanted = jnp.stack(known, axis=1).astype(jnp.float32)
+            received, rows, rows_known = exchange(depth, notes, rows, (wanted, policy_table.T))
+            policy_rows.append(rows_known)
         if depth == 0:
             first = [
                 received[:, k * capacity : (k + 1) * capacity] for k in range(2 * LEVELS)
             ]
             received = received[:, 2 * LEVELS * capacity :]
+            known = [(part % HALF).reshape(-1) for part in first[LEVELS:]]
         lineage = [
             received[:, k * capacity : (k + 1) * capacity] for k in range(len(lineage))
         ]
@@ -371,12 +376,14 @@
         columns += path[1:]
         counts = jnp.where(kept, first[LEVELS + depth] // HALF, 0).reshape(-1)
         path = [part.reshape(-1) for part in path]
+        if depth > 0:
+            known = path[1:2]
         lineage = [path[0] + HALF * path[1]] + path[2:]
         notes = []
     roots = rows.reshape(-1, rows.shape[-1])
     index = jnp.stack([part.reshape(-1) for part in columns + root_columns], axis=1)
     values = rebuild(
-        index.astype(jnp.float32), policy_rows, roots, policy_table.T, value_in, value_out.T
+        index.astype(jnp.float32), *policy_rows, roots, policy_table.T, value_in, value_out.T
     )
     return jnp.swapaxes(values, 1, 2)
 

time: 96.4 us -> 94.9 us (0.984)
  Pallas kernels: 73.3 us -> 70.5 us
  local copies, waits for them, and re-layouts: 10.4 us -> 11.7 us
    pallas_call x1, Pallas kernels: 36.7 us -> 33.8 us  [rebuild(): pl.pallas_call(rebuild_kernel, grid=(steps,), out_shape=jax.ShapeDtypeStr...]
    unnamed x6 -> x8, local copies, waits for them, and re-layouts: 3.88 us -> 5 us
where the time goes in v3:
time: 94.9 us; the launch traced here: 94.5 us
  Pallas kernels  70.5 us (74%)
  local copies, waits for them, and re-layouts  11.7 us (12%)
  other arithmetic  9.19 us (10%)
  between operations  2.33 us (2%)
    pallas_call x3, Pallas kernels, exchange(): pl.pallas_call(functools.partial(exchange_kernel, devices, stage), out_sh...  36.7 us
    pallas_call x1, Pallas kernels, rebuild(): pl.pallas_call(rebuild_kernel, grid=(steps,), out_shape=jax.ShapeDtypeStr...  33.8 us
    reduce_sum x4, other arithmetic, pick(): return jnp.sum(jnp.where(onehot, values[None, None, :], 0), axis=2)  5.46 us
    unnamed x8, local copies, waits for them, and re-layouts  5 us

profile of v3, /device:TPU:0, one launch (start us, length us, event | category | flops | bytes accessed | tf_op | source)
XLA Modules:
  0.0 94.5 jit_solution(8159576571184089349)
XLA Ops:
  0.0 0.8 multiply_add_fusion.2
  0.8 0.8 fusion.45
  1.7 0.7 copy.38
  2.4 0.5 slice.118
  3.6 0.1 reduce
  3.7 0.7 sub.78
  4.4 0.3 fusion.5
  4.6 0.3 fusion.1
  4.9 0.3 fusion.3
  5.2 3.4 %select_reduce_fusion.3 = (s32[32,16]{1,0:T(8,128)S(1)}, s32[32,16]{1,0:T(8,128)S(1)}, s32[32,16]{1,0:T(8,128)S(1)}, s32[32,16]{1,0:T(8,128)S(1)}, s32[32,16]{1,0:T(8,128)S(1)}, /*index=5*/s32[32,16]{1,0:T(8,128)S(1)}) fusion(s32[512]{0:T(512)S(1)} %bitcast.52, s32[32,512]{1,0:T(8,128)S(1)} %fusion.1, s32[512]{0:T(512)S(1)} %iota_add_fusion, ...), kind=kLoop, calls=%fused_computation.12 | loop fusion | flops 3929088 | bytes 217088 | tf_op jit(solution)/shard_map/reduce_sum | solution.py:32
  8.6 0.1 select_reduce_fusion.9
  8.8 0.1 concatenate.9
  9.0 0.8 copy-done.3
  9.7 12.6 %shard_map.82 = (s32[32,1,128]{2,1,0:T(1,128)S(1)}, bf16[4,16,1326]{2,1,0:T(8,128)(2,1)S(1)}) custom-call(s32[32,1,128]{2,1,0:T(1,128)S(1)} %bitcast.45, bf16[16,1326]{1,0:T(8,128)(2,1)S(1)} %copy-done.3), custom_call_target="tpu_custom_call" | custom-call | tf_op jit(solution)/shard_map/pallas_call | solution.py:301
  22.5 0.2 slice_reduce_fusion.4
  22.7 0.1 add_select_fusion.6
  22.8 0.1 stack_reshape.33
  23.1 0.1 reshape.205
  23.2 0.1 reshape.203
  23.3 0.3 reduce-window.34
  23.7 0.1 slice_reduce_fusion.1
  23.9 0.6 slice.105
  25.1 0.1 multiply_add_fusion.1
  25.2 0.1 add.201
  25.3 0.7 select_reduce_fusion.2
  26.0 0.1 stack_reshape.31
  26.1 0.1 copy.42.refs_2_
  26.3 15.8 %shard_map.83 = (s32[32,1,128]{2,1,0:T(1,128)S(1)}, bf16[4,4,16,1326]{3,2,1,0:T(8,128)(2,1)S(1)}, bf16[3,512,1326]{2,1,0:T(8,128)(2,1)S(1)}) custom-call(s32[32,1,128]{2,1,0:T(1,128)S(1)} %bitcast.43, bf16[4,16,1326]{2,1,0:T(8,128)(2,1)S(1)} %get-tuple-element.14.refs_1_, f32[512,3]{1,0:T(8,128)S(1)} %copy.42.refs_2_, bf16[1326,2048]{1,0:T(8,128)(2,1)} %bitcast.46), custom_call_target="tpu_custom_call" | custom-call | tf_op jit(solution)/shard_map/pallas_call | solution.py:301
  42.1 2.0 %copy-done = bf16[3,512,1326]{2,1,0:T(8,128)(2,1)} copy-done((bf16[3,512,1326]{2,1,0:T(8,128)(2,1)}, bf16[3,512,1326]{2,1,0:T(8,128)(2,1)S(1)}, u32[]{:S(2)}) %copy-start) | copy-done | bytes 4073496
  44.2 0.2 slice_reduce_fusion.3
  44.4 0.1 fusion.33
  44.5 0.1 stack_reshape.38
  44.7 0.3 reduce-window.39
  45.1 0.1 slice_reduce_fusion
  45.3 0.6 slice.113
  46.7 0.1 add.209
  46.8 1.3 %select_reduce_fusion.1 = (s32[32,16]{1,0:T(8,128)S(1)}, s32[32,16]{1,0:T(8,128)S(1)}) fusion(s32[512]{0:T(512)S(1)} %add.209, s32[512]{0:T(512)S(1)} %get-tuple-element.40, s32[32,16]{1,0:T(8,128)S(1)} %get-tuple-element.68, s32[512]{0:T(512)S(1)} %get-tuple-element.39, s32[512]{0:T(512)S(1)} %broadcast_in_dim.154), kind=kLoop, calls=%fused_computation.10 | loop fusion | flops 1833984 | bytes 14336 | tf_op jit(solution)/shard_map/reduce_sum | solution.py:32
  48.2 0.2 copy.43.refs_2_
  48.3 8.3 %shard_map.84 = (s32[32,1,128]{2,1,0:T(1,128)S(1)}, bf16[2,4,4,16,1326]{4,3,2,1,0:T(8,128)(2,1)S(1)}, bf16[1,512,1326]{2,1,0:T(8,128)(2,1)S(1)}) custom-call(s32[32,1,128]{2,1,0:T(1,128)S(1)} %bitcast.44, bf16[4,4,16,1326]{3,2,1,0:T(8,128)(2,1)S(1)} %get-tuple-element.16.refs_1_, f32[512,1]{1,0:T(8,128)S(1)} %copy.43.refs_2_, bf16[1326,2048]{1,0:T(8,128)(2,1)} %bitcast.47), custom_call_target="tpu_custom_call" | custom-call | tf_op jit(solution)/shard_map/pallas_call | solution.py:301
  56.7 1.1 %copy-done.1 = bf16[2,4,4,16,1326]{4,3,2,1,0:T(8,128)(2,1)} copy-done((bf16[2,4,4,16,1326]{4,3,2,1,0:T(8,128)(2,1)}, bf16[2,4,4,16,1326]{4,3,2,1,0:T(8,128)(2,1)S(1)}, u32[]{:S(2)}) %copy-start.1) | copy-done | bytes 1357848
  57.8 1.1 %copy-done.2 = bf16[1,512,1326]{2,1,0:T(8,128)(2,1)} copy-done((bf16[1,512,1326]{2,1,0:T(8,128)(2,1)}, bf16[1,512,1326]{2,1,0:T(8,128)(2,1)S(1)}, u32[]{:S(2)}) %copy-start.2) | copy-done | bytes 1357848
  59.1 0.2 slice_reduce_fusion.2
  59.3 0.1 fusion.25
  59.4 0.1 stack_reshape.39
  59.5 0.1 stack_reshape.35
  59.5 0.1 stack_reshape.36
  59.7 0.9 copy.44.index_ref
  60.6 33.8 %shard_map.85 = bf16[3,1326,512]{2,1,0:T(8,128)(2,1)} custom-call(f32[512,9]{1,0:T(8,128)} %copy.44.index_ref, bf16[3,512,1326]{2,1,0:T(8,128)(2,1)} %copy-done, bf16[1,512,1326]{2,1,0:T(8,128)(2,1)} %copy-done.2, bf16[512,1326]{1,0:T(8,128)(2,1)} %bitcast.34, bf16[1326,2048]{1,0:T(8,128)(2,1)} %bitcast.48, bf16[1326,1536]{1,0:T(8,128)(2,1)} %in_hbm.1, ...), custom_call_target="tpu_custom_call" | custom-call | tf_op jit(solution)/shard_map/pallas_call | solution.py:154
  (42 shorter events, 1.7 us)
Async XLA Ops:
  9.0 0.8 copy-start.3
  42.1 2.0 %copy-start = (bf16[3,512,1326]{2,1,0:T(8,128)(2,1)}, bf16[3,512,1326]{2,1,0:T(8,128)(2,1)S(1)}, u32[]{:S(2)}) copy-start(bf16[3,512,1326]{2,1,0:T(8,128)(2,1)S(1)} %get-tuple-element.18.policy_ref) | copy-start | bytes 12220420
  56.7 1.1 %copy-start.1 = (bf16[2,4,4,16,1326]{4,3,2,1,0:T(8,128)(2,1)}, bf16[2,4,4,16,1326]{4,3,2,1,0:T(8,128)(2,1)S(1)}, u32[]{:S(2)}) copy-start(bf16[2,4,4,16,1326]{4,3,2,1,0:T(8,128)(2,1)S(1)} %get-tuple-element.20) | copy-start | bytes 4073476
  57.8 1.1 %copy-start.2 = (bf16[1,512,1326]{2,1,0:T(8,128)(2,1)}, bf16[1,512,1326]{2,1,0:T(8,128)(2,1)S(1)}, u32[]{:S(2)}) copy-start(bf16[1,512,1326]{2,1,0:T(8,128)(2,1)S(1)} %get-tuple-element.19.second_ref) | copy-start | bytes 4073476

commit v4 on v3

--- a/solution.py
+++ b/solution.py
@@ -167,7 +167,7 @@
         ]
         + [pltpu.VMEM((rows, hands), jnp.bfloat16)] * 2
         + [pltpu.SemaphoreType.DMA((4,))],
-        compiler_params=pltpu.CompilerParams(vmem_limit_bytes=56 * 1024 * 1024),
+        compiler_params=pltpu.CompilerParams(vmem_limit_bytes=52 * 1024 * 1024),
     )(index, policy_rows, second_rows, roots, table, value_in, value_out)
 
 

time: 94.9 us -> 92.7 us (0.977)
  local copies, waits for them, and re-layouts: 11.7 us -> 9.83 us
    unnamed x8 -> x6, local copies, waits for them, and re-layouts: 5 us -> 3.88 us
where the time goes in v4:
time: 92.7 us; the launch traced here: 92.3 us
  Pallas kernels  70.2 us (76%)
  local copies, waits for them, and re-layouts  9.83 us (11%)
  other arithmetic  9.19 us (10%)
  between operations  2.34 us (3%)
    pallas_call x3, Pallas kernels, exchange(): pl.pallas_call(functools.partial(exchange_kernel, devices, stage), out_sh...  36.7 us
    pallas_call x1, Pallas kernels, rebuild(): pl.pallas_call(rebuild_kernel, grid=(steps,), out_shape=jax.ShapeDtypeStr...  33.5 us
    reduce_sum x4, other arithmetic, pick(): return jnp.sum(jnp.where(onehot, values[None, None, :], 0), axis=2)  5.46 us
    unnamed x6, local copies, waits for them, and re-layouts  3.88 us

profile of v4, /device:TPU:0, one launch (start us, length us, event | category | flops | bytes accessed | tf_op | source)
XLA Modules:
  0.0 92.3 jit_solution(17411018151615635914)
XLA Ops:
  0.0 0.8 multiply_add_fusion.2
  0.8 0.8 fusion.45
  1.7 0.7 copy.38
  2.4 0.5 slice.118
  3.6 0.1 reduce
  3.7 0.7 sub.78
  4.4 0.3 fusion.5
  4.6 0.3 fusion.1
  4.9 0.3 fusion.3
  5.2 3.4 %select_reduce_fusion.3 = (s32[32,16]{1,0:T(8,128)S(1)}, s32[32,16]{1,0:T(8,128)S(1)}, s32[32,16]{1,0:T(8,128)S(1)}, s32[32,16]{1,0:T(8,128)S(1)}, s32[32,16]{1,0:T(8,128)S(1)}, /*index=5*/s32[32,16]{1,0:T(8,128)S(1)}) fusion(s32[512]{0:T(512)S(1)} %bitcast.52, s32[32,512]{1,0:T(8,128)S(1)} %fusion.1, s32[512]{0:T(512)S(1)} %iota_add_fusion, ...), kind=kLoop, calls=%fused_computation.12 | loop fusion | flops 3929088 | bytes 217088 | tf_op jit(solution)/shard_map/reduce_sum | solution.py:32
  8.6 0.1 select_reduce_fusion.9
  8.8 0.1 concatenate.9
  9.0 0.8 copy-done.2
  9.7 12.6 %shard_map.82 = (s32[32,1,128]{2,1,0:T(1,128)S(1)}, bf16[4,16,1326]{2,1,0:T(8,128)(2,1)S(1)}) custom-call(s32[32,1,128]{2,1,0:T(1,128)S(1)} %bitcast.45, bf16[16,1326]{1,0:T(8,128)(2,1)S(1)} %copy-done.2), custom_call_target="tpu_custom_call" | custom-call | tf_op jit(solution)/shard_map/pallas_call | solution.py:301
  22.5 0.2 slice_reduce_fusion.4
  22.7 0.1 add_select_fusion.6
  22.8 0.1 stack_reshape.33
  22.9 0.1 stack_reshape.32
  23.0 0.1 stack_reshape.37
  23.1 0.1 reshape.205
  23.2 0.1 reshape.203
  23.3 0.3 reduce-window.34
  23.7 0.1 slice_reduce_fusion.1
  23.9 0.6 slice.105
  25.1 0.1 multiply_add_fusion.1
  25.3 0.7 select_reduce_fusion.2
  26.0 0.1 stack_reshape.31
  26.1 0.1 copy.42.refs_2_
  26.3 15.8 %shard_map.83 = (s32[32,1,128]{2,1,0:T(1,128)S(1)}, bf16[4,4,16,1326]{3,2,1,0:T(8,128)(2,1)S(1)}, bf16[3,512,1326]{2,1,0:T(8,128)(2,1)S(1)}) custom-call(s32[32,1,128]{2,1,0:T(1,128)S(1)} %bitcast.43, bf16[4,16,1326]{2,1,0:T(8,128)(2,1)S(1)} %get-tuple-element.14.refs_1_, f32[512,3]{1,0:T(8,128)S(1)} %copy.42.refs_2_, bf16[1326,2048]{1,0:T(8,128)(2,1)} %bitcast.46), custom_call_target="tpu_custom_call" | custom-call | tf_op jit(solution)/shard_map/pallas_call | solution.py:301
  42.1 2.0 %copy-done = bf16[3,512,1326]{2,1,0:T(8,128)(2,1)} copy-done((bf16[3,512,1326]{2,1,0:T(8,128)(2,1)}, bf16[3,512,1326]{2,1,0:T(8,128)(2,1)S(1)}, u32[]{:S(2)}) %copy-start) | copy-done | bytes 4073496
  44.2 0.2 slice_reduce_fusion.3
  44.4 0.1 fusion.33
  44.5 0.1 stack_reshape.38
  44.7 0.3 reduce-window.39
  45.1 0.1 slice_reduce_fusion
  45.3 0.6 slice.113
  46.7 0.1 add.209
  46.8 1.3 %select_reduce_fusion.1 = (s32[32,16]{1,0:T(8,128)S(1)}, s32[32,16]{1,0:T(8,128)S(1)}) fusion(s32[512]{0:T(512)S(1)} %add.209, s32[512]{0:T(512)S(1)} %get-tuple-element.40, s32[32,16]{1,0:T(8,128)S(1)} %get-tuple-element.68, s32[512]{0:T(512)S(1)} %get-tuple-element.39, s32[512]{0:T(512)S(1)} %broadcast_in_dim.154), kind=kLoop, calls=%fused_computation.10 | loop fusion | flops 1833984 | bytes 14336 | tf_op jit(solution)/shard_map/reduce_sum | solution.py:32
  48.2 0.2 copy.43.refs_2_
  48.3 8.3 %shard_map.84 = (s32[32,1,128]{2,1,0:T(1,128)S(1)}, bf16[2,4,4,16,1326]{4,3,2,1,0:T(8,128)(2,1)S(1)}, bf16[1,512,1326]{2,1,0:T(8,128)(2,1)S(1)}) custom-call(s32[32,1,128]{2,1,0:T(1,128)S(1)} %bitcast.44, bf16[4,4,16,1326]{3,2,1,0:T(8,128)(2,1)S(1)} %get-tuple-element.16.refs_1_, f32[512,1]{1,0:T(8,128)S(1)} %copy.43.refs_2_, bf16[1326,2048]{1,0:T(8,128)(2,1)} %bitcast.47), custom_call_target="tpu_custom_call" | custom-call | tf_op jit(solution)/shard_map/pallas_call | solution.py:301
  56.7 1.1 %copy-done.1 = bf16[2,4,4,16,1326]{4,3,2,1,0:T(8,128)(2,1)} copy-done((bf16[2,4,4,16,1326]{4,3,2,1,0:T(8,128)(2,1)}, bf16[2,4,4,16,1326]{4,3,2,1,0:T(8,128)(2,1)S(1)}, u32[]{:S(2)}) %copy-start.1) | copy-done | bytes 1357848
  58.0 0.2 slice_reduce_fusion.2
  58.1 0.1 fusion.25
  58.2 0.1 stack_reshape.39
  58.3 0.1 stack_reshape.35
  58.4 0.1 stack_reshape.36
  58.6 0.1 copy.44.index_ref
  58.7 33.5 %shard_map.85 = bf16[3,1326,512]{2,1,0:T(8,128)(2,1)} custom-call(f32[512,9]{1,0:T(8,128)S(1)} %copy.44.index_ref, bf16[3,512,1326]{2,1,0:T(8,128)(2,1)} %copy-done, bf16[1,512,1326]{2,1,0:T(8,128)(2,1)S(1)} %get-tuple-element.19.second_ref, bf16[512,1326]{1,0:T(8,128)(2,1)} %bitcast.34, bf16[1326,2048]{1,0:T(8,128)(2,1)} %bitcast.48, ...), custom_call_target="tpu_custom_call" | custom-call | tf_op jit(solution)/shard_map/pallas_call | solution.py:154
  (40 shorter events, 1.6 us)
Async XLA Ops:
  9.0 0.8 copy-start.2
  42.1 2.0 %copy-start = (bf16[3,512,1326]{2,1,0:T(8,128)(2,1)}, bf16[3,512,1326]{2,1,0:T(8,128)(2,1)S(1)}, u32[]{:S(2)}) copy-start(bf16[3,512,1326]{2,1,0:T(8,128)(2,1)S(1)} %get-tuple-element.18.policy_ref) | copy-start | bytes 12220420
  56.7 1.1 %copy-start.1 = (bf16[2,4,4,16,1326]{4,3,2,1,0:T(8,128)(2,1)}, bf16[2,4,4,16,1326]{4,3,2,1,0:T(8,128)(2,1)S(1)}, u32[]{:S(2)}) copy-start(bf16[2,4,4,16,1326]{4,3,2,1,0:T(8,128)(2,1)S(1)} %get-tuple-element.20) | copy-start | bytes 4073476
